TPU v7x, 32 devices: a whole 2x2x4 slice. The times are simulated.
32 devices in a mesh: dp: 8 (over z, y), tensor: 4 (over x, core).
Axes of the slice: x: 2, y: 2, z: 4, core: 2. Of those that a mesh axis runs over, the one named last changes fastest.
Arguments:
- query_act: bfloat16 [8, 1024, 1024], P('dp', None, 'tensor'), may hold values from -6 to 6
- rotated_keys: bfloat16 [8, 1024, 256], P('dp'), may hold values from -6 to 6
- value_input: bfloat16 [8, 1024, 256], P('dp'), may hold values from -6 to 6
- grad_out: bfloat16 [8, 1024, 8192], P('dp', 'tensor'), may hold values from -6 to 6
- out_weight: bfloat16 [1024, 8192], P('tensor', 'dp'), may hold values from -0.1875 to 0.1875
- doc_lengths: int32 [8, 4], P('dp'), may hold values from 1 to 512, 1024 in all within a row
Outputs:
- query_grad: bfloat16 [8, 1024, 1024], P('dp', None, 'tensor')
- key_gradient: bfloat16 [8, 4, 512, 128], P('dp', 'tensor')
- value_gradient: bfloat16 [8, 4, 512, 128], P('dp', 'tensor')
- weight_grad: float32 [1024, 8192], P('tensor', 'dp')
All inputs are finite; a program needn't handle non-finite values.
Results may differ from a plain program's by a relative error of at most 0.015.
The roundings to bfloat16 on the way count: a program that leaves them out, or rounds other values in their place, can miss the bound.
Values may be sent and summed in bfloat16 or wider, within the bound.
A program may use at most 128 MiB of HBM per device.

v0:
```python
import jax
import jax.numpy as jnp
from jax import lax
from jax.sharding import PartitionSpec as P

HEAD_SIZE = 128


def swapped(value, axis, apart):
    mask = 2**apart
    pairs = [(source, source ^ mask) for source in range(lax.axis_size(axis))]
    return lax.ppermute(value, axis, pairs)


def shards(query_act, rotated_keys, value_input, grad_out, out_weight, doc_lengths):
    score_scale = HEAD_SIZE ** (-0.5)
    tensor_index = lax.axis_index("tensor")
    kv_group = tensor_index // 2
    own_half = tensor_index % 2
    seq_len = query_act.shape[1]
    head_count = query_act.shape[2] // HEAD_SIZE
    query_heads = query_act[0].reshape(seq_len, head_count, HEAD_SIZE).transpose(1, 0, 2)
    key_rows = lax.dynamic_slice_in_dim(rotated_keys[0], kv_group * HEAD_SIZE, HEAD_SIZE, 1)
    value_rows = lax.dynamic_slice_in_dim(value_input[0], kv_group * HEAD_SIZE, HEAD_SIZE, 1)
    doc_ends = jnp.cumsum(doc_lengths[0])
    positions = jnp.arange(seq_len, dtype=jnp.int32)
    doc_ids = jnp.sum((positions[:, None] >= doc_ends[None, :]).astype(jnp.int32), axis=1)
    block_rows = min(512, seq_len)
    block_count = seq_len // block_rows
    full_weight = lax.all_gather(out_weight, "dp", axis=1, tiled=True)

    def key_reach():
        return seq_len

    def masked_scores(block_idx, key_span):
        first = block_idx * block_rows
        query_block = query_heads[:, first : first + block_rows]
        scores = (
            jnp.einsum("hqd,kd->hqk", query_block, key_rows, preferred_element_type=jnp.float32)
            * score_scale
        )
        allowed = (positions[None, :key_span] <= positions[first : first + block_rows, None]) & (
            doc_ids[None, :key_span] == doc_ids[first : first + block_rows, None]
        )
        return jnp.where(allowed[None], scores, -jnp.inf)

    totals_list = []
    outputs_list = []
    for block_idx in range(block_count):
        key_span = key_reach()
        scores = masked_scores(block_idx, key_span)
        row_max = jnp.max(scores, axis=-1, keepdims=True)
        log_total = row_max + jnp.log(jnp.sum(jnp.exp(scores - row_max), axis=-1, keepdims=True))
        prob_bf16 = jnp.exp(scores - log_total).astype(jnp.bfloat16)
        outputs_list.append(
            jnp.einsum(
                "hqk,kd->hqd", prob_bf16, value_rows, preferred_element_type=jnp.float32
            ).astype(jnp.bfloat16)
        )
        totals_list.append(log_total)
    attn_out = jnp.concatenate(outputs_list, axis=1)
    out_flat = attn_out.transpose(1, 0, 2).reshape(seq_len, head_count * HEAD_SIZE)
    local_rows = grad_out[0]
    gathered = lax.all_gather(local_rows, "tensor", axis=0, tiled=True)
    out_grad = jnp.einsum(
        "sd,hd->sh", gathered, full_weight, preferred_element_type=jnp.float32
    ).astype(jnp.bfloat16)
    weight_part = jnp.einsum("sh,sd->hd", out_flat, gathered, preferred_element_type=jnp.float32)
    weight_grad = lax.psum_scatter(weight_part, "dp", scatter_dimension=1, tiled=True)
    grad_heads = out_grad.reshape(seq_len, head_count, HEAD_SIZE).transpose(1, 0, 2)
    key_accum = jnp.zeros((seq_len, HEAD_SIZE), jnp.float32)
    value_accum = jnp.zeros((seq_len, HEAD_SIZE), jnp.float32)
    query_list = []
    for block_idx in range(block_count):
        key_span = key_reach()
        first = block_idx * block_rows
        scores = masked_scores(block_idx, key_span)
        prob_block = jnp.exp(scores - totals_list[block_idx])
        prob_bf16 = prob_block.astype(jnp.bfloat16)
        grad_block = grad_heads[:, first : first + block_rows]
        out_block = attn_out[:, first : first + block_rows]
        query_block = query_heads[:, first : first + block_rows]
        dprobs = jnp.einsum(
            "hqd,kd->hqk", grad_block, value_rows, preferred_element_type=jnp.float32
        )
        row_delta = jnp.sum(
            grad_block.astype(jnp.float32) * out_block.astype(jnp.float32), axis=-1, keepdims=True
        )
        score_gradient = (prob_block * (dprobs - row_delta) * score_scale).astype(jnp.bfloat16)
        query_list.append(
            jnp.einsum(
                "hqk,kd->hqd", score_gradient, key_rows, preferred_element_type=jnp.float32
            ).astype(jnp.bfloat16)
        )
        key_accum = key_accum.at[:key_span].add(
            jnp.einsum(
                "hqk,hqd->kd", score_gradient, query_block, preferred_element_type=jnp.float32
            )
        )
        value_accum = value_accum.at[:key_span].add(
            jnp.einsum("hqk,hqd->kd", prob_bf16, grad_block, preferred_element_type=jnp.float32)
        )
    query_grad = (
        jnp.concatenate(query_list, axis=1)
        .transpose(1, 0, 2)
        .reshape(1, seq_len, head_count * HEAD_SIZE)
    )
    half_rows = seq_len // 2
    other_start = (1 - own_half) * half_rows
    outgoing = (
        lax.dynamic_slice_in_dim(key_accum, other_start, half_rows, 0),
        lax.dynamic_slice_in_dim(value_accum, other_start, half_rows, 0),
    )
    partner = swapped((outgoing[0], outgoing[1]), "tensor", 0)
    key_mine = lax.dynamic_slice_in_dim(key_accum, own_half * half_rows, half_rows, 0) + partner[0]
    value_mine = (
        lax.dynamic_slice_in_dim(value_accum, own_half * half_rows, half_rows, 0) + partner[1]
    )
    key_gradient = key_mine.astype(jnp.bfloat16).reshape(1, 1, half_rows, HEAD_SIZE)
    value_gradient = value_mine.astype(jnp.bfloat16).reshape(1, 1, half_rows, HEAD_SIZE)
    return (query_grad, key_gradient, value_gradient, weight_grad)


def solution(mesh):
    placed = (
        P("dp", None, "tensor"),
        P("dp", None, None),
        P("dp", None, None),
        P("dp", "tensor", None),
        P("tensor", "dp"),
        P("dp", None),
    )
    return jax.shard_map(
        shards,
        mesh=mesh,
        in_specs=placed,
        out_specs=(
            P("dp", None, "tensor"),
            P("dp", "tensor", None, None),
            P("dp", "tensor", None, None),
            P("tensor", "dp"),
        ),
        check_vma=False,
    )
```

profile of v0, /device:TPU:0, one launch (start us, length us, event | category | flops | bytes accessed | tf_op | source)
XLA Modules:
  0.0 374.6 jit_solution(8681585686457070649)
XLA Ops:
  8.0 0.7 all-gather.6.cloned.1.call-update
  9.6 0.9 fusion.9
  10.5 0.9 fusion.7
  11.4 0.9 fusion.6
  12.4 2.2 exponential_reduce_fusion
  14.7 1.6 convolution_convert_fusion.1
  16.2 69.5 %all-gather.4.cloned.1.call-done = bf16[256,8192]{1,0:T(8,128)(2,1)} async-done(((bf16[256,1024]{1,0:T(8,128)(2,1)}), bf16[256,8192]{1,0:T(8,128)(2,1)}) %all-gather.4.cloned.1.call-update) | async-done | bytes 4194320 | tf_op jit(solution)/shard_map/all_gather | solution.py:30
  85.7 106.0 %all-gather.6.cloned.1.call-done = bf16[1,1024,8192]{2,1,0:T(8,128)(2,1)} async-done(((bf16[1,256,8192]{2,1,0:T(8,128)(2,1)}), bf16[1,1024,8192]{2,1,0:T(8,128)(2,1)}) %all-gather.6.cloned.1.call-update) | async-done | bytes 16777232 | tf_op jit(solution)/shard_map/all_gather | solution.py:64
  191.8 11.5 %fusion.10 = bf16[1024,256]{0,1:T(8,128)(2,1)S(1)} fusion(bf16[256,8192]{1,0:T(8,128)(2,1)} %all-gather.4.cloned.1.call-done, bf16[1,1024,8192]{2,1,0:T(8,128)(2,1)} %all-gather.6.cloned.1.call-done), kind=kOutput, calls=%fused_computation.20 | convolution fusion | flops 4295229440 | bytes 21495808 | tf_op jit(solution)/shard_map/sd,hd->sh/dot_general | solution.py:65
  203.5 3.8 %multiply_reduce_fusion.1 = (f32[2,512]{1,0:T(2,128)S(1)}, f32[2,512]{1,0:T(2,128)S(1)}, bf16[2,512,128]{2,1,0:T(8,128)(2,1)S(1)}) fusion(bf16[2,1024,128]{2,1,0:T(8,128)(2,1)S(1)} %bitcast.100, bf16[2,512,128]{2,1,0:T(8,128)(2,1)S(1)} %convolution_convert_fusion.1, bf16[1,1024,256]{2,1,0:T(8,128)(2,1)S(1)} %copy-done, s32[]{:T(128)S(6)} %select_n.33, ...), kind=kOutput, calls=%fused_computation.34 | convolution fusion | flops 273807360 | bytes 6041604 | tf_op jit(solution)/shard_map/hqk,kd->hqd/dot_general | solution.py:56
  207.6 12.5 %fusion = f32[256,8192]{1,0:T(8,128)} fusion(bf16[1024,256]{0,1:T(8,128)(2,1)S(1)} %bitcast.93, bf16[1,1024,8192]{2,1,0:T(8,128)(2,1)} %all-gather.6.cloned.1.call-done), kind=kOutput, calls=%fused_computation | convolution fusion | flops 4294967296 | bytes 25690112 | tf_op jit(solution)/shard_map/sh,sd->hd/dot_general | solution.py:68
  220.1 1.0 copy-done.7
  221.1 4.0 %multiply_convert_fusion = bf16[2,512,1024]{1,2,0:T(8,128)(2,1)S(1)} fusion(f32[1024,2,512]{2,0,1:T(8,128)} %copy-done.1, f32[2,512]{1,0:T(2,128)S(1)} %get-tuple-element.93, f32[2,512]{1,0:T(2,128)S(1)} %log_add_fusion, pred[512,1024]{0,1:T(8,128)(4,1)S(1)} %get-tuple-element.94, bf16[2,1024,128]{2,1,0:T(8,128)(2,1)S(1)} %bitcast.101, ...), kind=kOutput, calls=%fused_computation.6 | convolution fusion | flops 275775488 | bytes 7348228 | tf_op jit(solution)/shard_map/hqd,kd->hqk/dot_general | solution.py:83
  225.1 0.7 convolution_bitcast_fusion.2
  225.8 1.7 multiply_convert_fusion.1
  227.5 0.7 fusion.13
  228.6 0.8 convolution_convert_fusion
  229.8 1.1 convolution_bitcast_fusion
  230.8 1.3 fusion.14
  232.1 0.8 convolution_convert_fusion.2
  233.5 1.0 copy.40
  234.5 0.7 fusion.41
  235.2 1.6 fusion.42
  236.8 131.3 %reduce-scatter.2.cloned.1.call-done = f32[256,1024]{1,0:T(8,128)} async-done(((f32[256,8192]{1,0:T(8,128)}), f32[256,1024]{1,0:T(8,128)}) %reduce-scatter.2.cloned.1.call-update) | async-done | bytes 1048592 | tf_op jit(solution)/shard_map/reduce_scatter | solution.py:69
  (48 shorter events, 3.6 us)
Async XLA Ops:
  7.2 7.5 %copy-start = (bf16[1,1024,256]{2,1,0:T(8,128)(2,1)S(1)}, bf16[1,1024,256]{2,1,0:T(8,128)(2,1)}, u32[]{:S(2)}) copy-start(bf16[1,1024,256]{2,1,0:T(8,128)(2,1)} %param.24) | copy-start | bytes 1572868
  7.2 1.6 copy-start.10
  7.2 1.8 copy-start.5
  7.2 3.3 copy-start.8
  7.2 78.5 %all-gather.4.cloned.1.call-start = ((), (), s32[]{:S(2)}) async-start(), calls=%async_computation.1 | async-start | bytes 4718592 | tf_op jit(solution)/shard_map/all_gather | solution.py:30
  7.9 183.8 %all-gather.6.cloned.1.call-start = ((), (), s32[]{:S(2)}) async-start(), calls=%async_computation.3 | async-start | bytes 20971520 | tf_op jit(solution)/shard_map/all_gather | solution.py:64
  8.7 359.4 %reduce-scatter.2.cloned.1.call-start = ((), (), s32[]{:S(2)}) async-start(), calls=%async_computation.2 | async-start | bytes 9437184 | tf_op jit(solution)/shard_map/reduce_scatter | solution.py:69
  11.4 3.2 copy-start.1
  12.4 2.3 copy-start.3
  203.5 3.8 %copy-start.6 = (bf16[1024,2,128]{2,0,1:T(8,128)(2,1)}, bf16[1024,2,128]{2,0,1:T(8,128)(2,1)S(1)}, u32[]{:S(2)}) copy-start(bf16[1024,2,128]{2,0,1:T(8,128)(2,1)S(1)} %copy.31) | copy-start | bytes 1572868
  220.1 1.0 copy-start.7
  221.1 4.7 %copy-start.4 = (f32[1024,2,512]{2,0,1:T(8,128)S(1)}, f32[1024,2,512]{2,0,1:T(8,128)}, u32[]{:S(2)}) copy-start(f32[1024,2,512]{2,0,1:T(8,128)} %copy-done.3) | copy-start | bytes 12582916
  225.8 2.8 copy-start.9
  227.5 2.3 copy-start.2
  228.3 6.2 %collective-permute-start = (f32[512,128]{1,0:T(8,128)S(1)}, f32[512,128]{1,0:T(8,128)S(1)}, u32[]{:S(2)}, u32[]{:S(2)}) collective-permute-start(f32[512,128]{1,0:T(8,128)S(1)} %constant_dynamic-slice_fusion.1), channel_id=1, source_target_pairs={{0,1},{1,0},{2,3},{3,2},{4,5},{5,4},{6,7},{7,6},{8,9},{9,8},{10,11... | collective-permute-start | bytes 786440 | tf_op jit(solution)/shard_map/ppermute | solution.py:12
  232.9 2.3 collective-permute-start.1
Sparse Core Ops, SparseCore 0:
  10.2 75.4 all-gather.3
  87.3 104.4 all-gather.5
  220.2 147.8 reduce-scatter.1
where the time goes:
time: 375 us
  waiting for transfers between devices  308 us (82%)
  matrix products  42.1 us (11%)
  between operations  14.1 us (4%)
  other arithmetic  5.72 us (2%)
  local copies, waits for them, and re-layouts  3.8 us (1%)
    reduce_scatter x1, waiting for transfers between devices, shards(): lax.psum_scatter(weight_part, 'dp', scatter_dimension=1, tiled=True)  131 us
    all_gather x1, waiting for transfers between devices, shards(): gathered = lax.all_gather(local_rows, 'tensor', axis=0, tiled=True)  106 us
    all_gather x1, waiting for transfers between devices, shards(): full_weight = lax.all_gather(out_weight, 'dp', axis=1, tiled=True)  69.5 us
    dot_general x1, matrix products, shards(): jnp.einsum('sh,sd->hd', out_flat, gathered, preferred_element_type=jnp.fl...  12.5 us
    dot_general x1, matrix products, shards(): jnp.einsum('sd,hd->sh', gathered, full_weight, preferred_element_type=jnp...  11.5 us
  transfers between devices with their start and end apart: 5, of which 3 were waited for; matrix products, arithmetic and copies ran while one was open for 6% of the time, Pallas kernels for 0%

commit v1 on v0

--- a/solution.py
+++ b/solution.py
@@ -4,6 +4,18 @@
 from jax.sharding import PartitionSpec as P
 
 HEAD_SIZE = 128
+
+
+def summed_around(x, axis, dim, term):
+    length, position, rows = (lax.axis_size(axis), lax.axis_index(axis), x.shape[dim])
+    forward = [(i, (i + 1) % length) for i in range(length)]
+    held, running = (x, None)
+    for lap in range(length):
+        following = lax.ppermute(held, axis, forward) if lap < length - 1 else None
+        take_in = term(held, (position - lap) % length * rows)
+        running = take_in if running is None else running + take_in
+        held = following
+    return running
 
 
 def swapped(value, axis, apart):
@@ -27,7 +39,6 @@
     doc_ids = jnp.sum((positions[:, None] >= doc_ends[None, :]).astype(jnp.int32), axis=1)
     block_rows = min(512, seq_len)
     block_count = seq_len // block_rows
-    full_weight = lax.all_gather(out_weight, "dp", axis=1, tiled=True)
 
     def key_reach():
         return seq_len
@@ -62,8 +73,16 @@
     out_flat = attn_out.transpose(1, 0, 2).reshape(seq_len, head_count * HEAD_SIZE)
     local_rows = grad_out[0]
     gathered = lax.all_gather(local_rows, "tensor", axis=0, tiled=True)
-    out_grad = jnp.einsum(
-        "sd,hd->sh", gathered, full_weight, preferred_element_type=jnp.float32
+    out_grad = summed_around(
+        out_weight,
+        "dp",
+        1,
+        lambda shard, at: jnp.einsum(
+            "sd,hd->sh",
+            lax.dynamic_slice_in_dim(gathered, at, shard.shape[1], axis=1),
+            shard,
+            preferred_element_type=jnp.float32,
+        ),
     ).astype(jnp.bfloat16)
     weight_part = jnp.einsum("sh,sd->hd", out_flat, gathered, preferred_element_type=jnp.float32)
     weight_grad = lax.psum_scatter(weight_part, "dp", scatter_dimension=1, tiled=True)

time: 375 us -> 308 us (0.82)
  waiting for transfers between devices: 308 us -> 227 us
  matrix products: 42.1 us -> 52.4 us
    all_gather x1, waiting for transfers between devices: 106 us -> 20.9 us  [shards(): gathered = lax.all_gather(local_rows, 'tensor', axis=0, tiled=True)]
    ppermute x0 -> x7, waiting for transfers between devices: none -> 74.4 us  [summed_around(): following = lax.ppermute(held, axis, forward) if lap < length - 1 else None]
    all_gather x1 -> x0, waiting for transfers between devices: 69.5 us -> none  [shards(): full_weight = lax.all_gather(out_weight, 'dp', axis=1, tiled=True)]
    dot_general x1 -> x8, matrix products: 11.5 us -> 17.3 us  [shards(): jnp.einsum('sd,hd->sh', lax.dynamic_slice_in_dim(gathered, at, shard.shap...]
  transfers between devices with their start and end apart: 5 -> 11, of which waited for: 3 -> 8; matrix products, arithmetic and copies ran while one was open for 6% -> 13% of each run, Pallas kernels for 0% -> 0%
where the time goes in v1:
time: 308 us
  waiting for transfers between devices  227 us (74%)
  matrix products  52.4 us (17%)
  between operations  14.6 us (5%)
  other arithmetic  5.53 us (2%)
  local copies, waits for them, and re-layouts  4.01 us (1%)
  starting transfers between devices  3.74 us (1%)
    reduce_scatter x1, waiting for transfers between devices, shards(): lax.psum_scatter(weight_part, 'dp', scatter_dimension=1, tiled=True)  131 us
    ppermute x7, waiting for transfers between devices, summed_around(): following = lax.ppermute(held, axis, forward) if lap < length - 1 else None  74.4 us
    all_gather x1, waiting for transfers between devices, shards(): gathered = lax.all_gather(local_rows, 'tensor', axis=0, tiled=True)  20.9 us
    dot_general x8, matrix products, shards(): jnp.einsum('sd,hd->sh', lax.dynamic_slice_in_dim(gathered, at, shard.shap...  17.3 us
    dot_general x1, matrix products, shards(): jnp.einsum('sh,sd->hd', out_flat, gathered, preferred_element_type=jnp.fl...  12.7 us
    dot_general x2, matrix products, shards(): jnp.einsum('hqk,kd->hqd', prob_bf16, value_rows, preferred_element_type=j...  7.51 us
  transfers between devices with their start and end apart: 11, of which 8 were waited for; matrix products, arithmetic and copies ran while one was open for 13% of the time, Pallas kernels for 0%

profile of v1, /device:TPU:0, one launch (start us, length us, event | category | flops | bytes accessed | tf_op | source)
XLA Modules:
  0.0 307.7 jit_solution(11136758762622145101)
XLA Ops:
  8.3 3.0 collective-permute-start
  11.3 15.0 %collective-permute-done = bf16[256,1024]{1,0:T(8,128)(2,1)S(1)} collective-permute-done((bf16[256,1024]{1,0:T(8,128)(2,1)S(1)}, bf16[256,1024]{1,0:T(8,128)(2,1)S(1)}, u32[]{:S(2)}, u32[]{:S(2)}) %collective-permute-start) | collective-permute-done | bytes 524320 | tf_op jit(solution)/shard_map/ppermute | solution.py:14
  27.0 15.1 %collective-permute-done.1 = bf16[256,1024]{1,0:T(8,128)(2,1)} collective-permute-done((bf16[256,1024]{1,0:T(8,128)(2,1)S(1)}, bf16[256,1024]{1,0:T(8,128)(2,1)}, u32[]{:S(2)}, u32[]{:S(2)}) %collective-permute-start.1) | collective-permute-done | bytes 524320 | tf_op jit(solution)/shard_map/ppermute | solution.py:14
  43.0 14.2 %collective-permute-done.2 = bf16[256,1024]{1,0:T(8,128)(2,1)S(1)} collective-permute-done((bf16[256,1024]{1,0:T(8,128)(2,1)}, bf16[256,1024]{1,0:T(8,128)(2,1)S(1)}, u32[]{:S(2)}, u32[]{:S(2)}) %collective-permute-start.2) | collective-permute-done | bytes 524320 | tf_op jit(solution)/shard_map/ppermute | solution.py:14
  57.3 1.9 fusion.5
  59.2 2.1 fusion.4
  61.2 10.1 %collective-permute-done.3 = bf16[256,1024]{1,0:T(8,128)(2,1)S(1)} collective-permute-done((bf16[256,1024]{1,0:T(8,128)(2,1)S(1)}, bf16[256,1024]{1,0:T(8,128)(2,1)S(1)}, u32[]{:S(2)}, u32[]{:S(2)}) %collective-permute-start.3) | collective-permute-done | bytes 524320 | tf_op jit(solution)/shard_map/ppermute | solution.py:14
  71.3 2.0 exponential_reduce_fusion
  73.4 11.3 %collective-permute-done.4 = bf16[256,1024]{1,0:T(8,128)(2,1)} collective-permute-done((bf16[256,1024]{1,0:T(8,128)(2,1)S(1)}, bf16[256,1024]{1,0:T(8,128)(2,1)}, u32[]{:S(2)}, u32[]{:S(2)}) %collective-permute-start.4) | collective-permute-done | bytes 524320 | tf_op jit(solution)/shard_map/ppermute | solution.py:14
  84.9 3.7 %convolution_convert_fusion.1 = bf16[2,512,128]{2,1,0:T(8,128)(2,1)S(1)} fusion(bf16[1,1024,256]{2,1,0:T(8,128)(2,1)S(1)} %copy-done, s32[]{:T(128)S(6)} %select_n.89, f32[1024,2,512]{2,0,1:T(8,128)} %copy-done.2, f32[2,512]{1,0:T(2,128)S(1)} %log_add_fusion, pred[512,1024]{0,1:T(8,128)(4,1)S(1)} %get-tuple-element.94), kind=kOutput, calls=%fused_computation.57 | convolution fusion | flops 272760832 | bytes 5246980 | tf_op jit(solution)/shard_map/hqk,kd->hqd/dot_general | solution.py:67
  88.6 8.8 %collective-permute-done.5 = bf16[256,1024]{1,0:T(8,128)(2,1)} collective-permute-done((bf16[256,1024]{1,0:T(8,128)(2,1)}, bf16[256,1024]{1,0:T(8,128)(2,1)}, u32[]{:S(2)}, u32[]{:S(2)}) %collective-permute-start.5) | collective-permute-done | bytes 524320 | tf_op jit(solution)/shard_map/ppermute | solution.py:14
  97.3 20.9 %all-gather.3.cloned.1.call-done = bf16[1,1024,8192]{2,1,0:T(8,128)(2,1)} async-done(((bf16[1,256,8192]{2,1,0:T(8,128)(2,1)}), bf16[1,1024,8192]{2,1,0:T(8,128)(2,1)}) %all-gather.3.cloned.1.call-update) | async-done | bytes 16777232 | tf_op jit(solution)/shard_map/all_gather | solution.py:75
  118.2 2.6 fusion.20
  120.8 2.9 fusion.32
  123.7 3.2 %fusion.35 = f32[1024,256]{0,1:T(8,128)S(1)} fusion(f32[1024,256]{0,1:T(8,128)S(1)} %fusion.32, bf16[256,1024]{1,0:T(8,128)(2,1)} %collective-permute-done.1, bf16[1,1024,8192]{2,1,0:T(8,128)(2,1)} %all-gather.3.cloned.1.call-done, s32[]{:T(128)S(6)} %select_n.96), kind=kOutput, calls=%fused_computation.43 | convolution fusion | flops 537133056 | bytes 4718596 | tf_op jit(solution)/shard_map/sd,hd->sh/dot_general | solution.py:80
  126.9 2.4 fusion.38
  130.1 1.9 fusion.44
  132.0 1.8 fusion.47
  133.8 1.8 fusion.53
  136.0 3.8 %multiply_reduce_fusion.1 = (f32[2,512]{1,0:T(2,128)S(1)}, f32[2,512]{1,0:T(2,128)S(1)}, bf16[2,512,128]{2,1,0:T(8,128)(2,1)S(1)}) fusion(bf16[2,1024,128]{2,1,0:T(8,128)(2,1)S(1)} %bitcast.144, bf16[2,512,128]{2,1,0:T(8,128)(2,1)S(1)} %convolution_convert_fusion.1, bf16[1,1024,256]{2,1,0:T(8,128)(2,1)S(1)} %copy-done, s32[]{:T(128)S(6)} %select_n.89, ...), kind=kOutput, calls=%fused_computation.63 | convolution fusion | flops 273807360 | bytes 6041604 | tf_op jit(solution)/shard_map/hqk,kd->hqd/dot_general | solution.py:67
  140.0 12.7 %fusion = f32[256,8192]{1,0:T(8,128)} fusion(bf16[1024,256]{0,1:T(8,128)(2,1)S(1)} %bitcast.136, bf16[1,1024,8192]{2,1,0:T(8,128)(2,1)} %all-gather.3.cloned.1.call-done), kind=kOutput, calls=%fused_computation | convolution fusion | flops 4294967296 | bytes 25690112 | tf_op jit(solution)/shard_map/sh,sd->hd/dot_general | solution.py:87
  153.8 4.0 %multiply_convert_fusion = bf16[2,512,1024]{1,2,0:T(8,128)(2,1)S(1)} fusion(f32[1024,2,512]{2,0,1:T(8,128)} %copy-done.2, f32[2,512]{1,0:T(2,128)S(1)} %get-tuple-element.93, f32[2,512]{1,0:T(2,128)S(1)} %log_add_fusion, pred[512,1024]{0,1:T(8,128)(4,1)S(1)} %get-tuple-element.94, bf16[2,1024,128]{2,1,0:T(8,128)(2,1)S(1)} %bitcast.145, ...), kind=kOutput, calls=%fused_computation.4 | convolution fusion | flops 275775488 | bytes 7348228 | tf_op jit(solution)/shard_map/hqd,kd->hqk/dot_general | solution.py:102
  158.5 1.7 multiply_convert_fusion.1
  169.5 131.3 %reduce-scatter.2.cloned.1.call-done = f32[256,1024]{1,0:T(8,128)} async-done(((f32[256,8192]{1,0:T(8,128)}), f32[256,1024]{1,0:T(8,128)}) %reduce-scatter.2.cloned.1.call-update) | async-done | bytes 1048592 | tf_op jit(solution)/shard_map/reduce_scatter | solution.py:88
  (72 shorter events, 15.1 us)
Async XLA Ops:
  7.2 77.7 %copy-start = (bf16[1,1024,256]{2,1,0:T(8,128)(2,1)S(1)}, bf16[1,1024,256]{2,1,0:T(8,128)(2,1)}, u32[]{:S(2)}) copy-start(bf16[1,1024,256]{2,1,0:T(8,128)(2,1)} %param.24) | copy-start | bytes 1572868
  7.2 1.1 copy-start.12
  7.2 19.0 %copy-start.13 = (s32[1,4]{1,0:T(1,128)S(1)}, s32[1,4]{1,0:T(1,128)}, u32[]{:S(2)}) copy-start(s32[1,4]{1,0:T(1,128)} %param.27) | copy-start | bytes 52
  7.2 19.2 %copy-start.8 = (bf16[1,1024,256]{2,1,0:T(8,128)(2,1)S(1)}, bf16[1,1024,256]{2,1,0:T(8,128)(2,1)}, u32[]{:S(2)}) copy-start(bf16[1,1024,256]{2,1,0:T(8,128)(2,1)} %param.22) | copy-start | bytes 1572868
  7.2 111.0 %all-gather.3.cloned.1.call-start = ((), (), s32[]{:S(2)}) async-start(), calls=%async_computation.2 | async-start | bytes 20971520 | tf_op jit(solution)/shard_map/all_gather | solution.py:75
  7.9 292.9 %reduce-scatter.2.cloned.1.call-start = ((), (), s32[]{:S(2)}) async-start(), calls=%async_computation.1 | async-start | bytes 9437184 | tf_op jit(solution)/shard_map/reduce_scatter | solution.py:88
  8.3 18.0 %collective-permute-start = (bf16[256,1024]{1,0:T(8,128)(2,1)S(1)}, bf16[256,1024]{1,0:T(8,128)(2,1)S(1)}, u32[]{:S(2)}, u32[]{:S(2)}) collective-permute-start(bf16[256,1024]{1,0:T(8,128)(2,1)S(1)} %copy-done.12), channel_id=1, source_target_pairs={{0,4},{4,8},{8,12},{12,16},{16,20},{20,24},{24,28},{28,0},{1,5},{5... | collective-permute-start | bytes 1572872 | tf_op jit(solution)/shard_map/ppermute | solution.py:14
  26.2 15.9 %collective-permute-start.1 = (bf16[256,1024]{1,0:T(8,128)(2,1)S(1)}, bf16[256,1024]{1,0:T(8,128)(2,1)}, u32[]{:S(2)}, u32[]{:S(2)}) collective-permute-start(bf16[256,1024]{1,0:T(8,128)(2,1)S(1)} %collective-permute-done), channel_id=1, source_target_pairs={{0,4},{4,8},{8,12},{12,16},{16,20},{20,24},{24,28},{28,0},{1,5},{5... | collective-permute-start | bytes 1572872 | tf_op jit(solution)/shard_map/ppermute | solution.py:14
  42.1 15.1 %collective-permute-start.2 = (bf16[256,1024]{1,0:T(8,128)(2,1)}, bf16[256,1024]{1,0:T(8,128)(2,1)S(1)}, u32[]{:S(2)}, u32[]{:S(2)}) collective-permute-start(bf16[256,1024]{1,0:T(8,128)(2,1)} %collective-permute-done.1), channel_id=1, source_target_pairs={{0,4},{4,8},{8,12},{12,16},{16,20},{20,24},{24,28},{28,0},{1,5},{5... | collective-permute-start | bytes 1572872 | tf_op jit(solution)/shard_map/ppermute | solution.py:14
  57.3 14.1 %collective-permute-start.3 = (bf16[256,1024]{1,0:T(8,128)(2,1)S(1)}, bf16[256,1024]{1,0:T(8,128)(2,1)S(1)}, u32[]{:S(2)}, u32[]{:S(2)}) collective-permute-start(bf16[256,1024]{1,0:T(8,128)(2,1)S(1)} %collective-permute-done.2), channel_id=1, source_target_pairs={{0,4},{4,8},{8,12},{12,16},{16,20},{20,24},{24,28},{28,0},{1,5},{5... | collective-permute-start | bytes 1572872 | tf_op jit(solution)/shard_map/ppermute | solution.py:14
  59.1 14.2 %copy-start.2 = (f32[1024,2,512]{2,0,1:T(8,128)}, f32[1024,2,512]{2,0,1:T(8,128)S(1)}, u32[]{:S(2)}) copy-start(f32[1024,2,512]{2,0,1:T(8,128)S(1)} %get-tuple-element.101) | copy-start | bytes 12582916
  61.2 12.1 %copy-start.4 = (f32[1024,2,512]{2,0,1:T(8,128)}, f32[1024,2,512]{2,0,1:T(8,128)S(1)}, u32[]{:S(2)}) copy-start(f32[1024,2,512]{2,0,1:T(8,128)S(1)} %get-tuple-element.99) | copy-start | bytes 12582916
  71.3 2.0 copy-start.6
  71.3 13.3 %collective-permute-start.4 = (bf16[256,1024]{1,0:T(8,128)(2,1)S(1)}, bf16[256,1024]{1,0:T(8,128)(2,1)}, u32[]{:S(2)}, u32[]{:S(2)}) collective-permute-start(bf16[256,1024]{1,0:T(8,128)(2,1)S(1)} %collective-permute-done.3), channel_id=1, source_target_pairs={{0,4},{4,8},{8,12},{12,16},{16,20},{20,24},{24,28},{28,0},{1,5},{5... | collective-permute-start | bytes 1572872 | tf_op jit(solution)/shard_map/ppermute | solution.py:14
  84.7 12.7 %collective-permute-start.5 = (bf16[256,1024]{1,0:T(8,128)(2,1)}, bf16[256,1024]{1,0:T(8,128)(2,1)}, u32[]{:S(2)}, u32[]{:S(2)}) collective-permute-start(bf16[256,1024]{1,0:T(8,128)(2,1)} %collective-permute-done.4), channel_id=1, source_target_pairs={{0,4},{4,8},{8,12},{12,16},{16,20},{20,24},{24,28},{28,0},{1,5},{5... | collective-permute-start | bytes 1572872 | tf_op jit(solution)/shard_map/ppermute | solution.py:14
  97.3 36.5 %collective-permute-start.6 = (bf16[256,1024]{1,0:T(8,128)(2,1)}, bf16[256,1024]{1,0:T(8,128)(2,1)}, u32[]{:S(2)}, u32[]{:S(2)}) collective-permute-start(bf16[256,1024]{1,0:T(8,128)(2,1)} %collective-permute-done.5), channel_id=1, source_target_pairs={{0,4},{4,8},{8,12},{12,16},{16,20},{20,24},{24,28},{28,0},{1,5},{5... | collective-permute-start | bytes 1572872 | tf_op jit(solution)/shard_map/ppermute | solution.py:14
  118.2 11.0 %copy-start.1 = (bf16[1,1024,8192]{2,1,0:T(8,128)(2,1)S(1)}, bf16[1,1024,8192]{2,1,0:T(8,128)(2,1)}, u32[]{:S(2)}) copy-start(bf16[1,1024,8192]{2,1,0:T(8,128)(2,1)} %all-gather.3.cloned.1.call-done) | copy-start | bytes 50331652
  123.7 5.6 %copy-start.7 = (bf16[256,1024]{1,0:T(8,128)(2,1)S(1)}, bf16[256,1024]{1,0:T(8,128)(2,1)}, u32[]{:S(2)}) copy-start(bf16[256,1024]{1,0:T(8,128)(2,1)} %copy-done.6) | copy-start | bytes 1572868
  136.0 3.8 %copy-start.9 = (bf16[1024,2,128]{2,0,1:T(8,128)(2,1)}, bf16[1024,2,128]{2,0,1:T(8,128)(2,1)S(1)}, u32[]{:S(2)}) copy-start(bf16[1024,2,128]{2,0,1:T(8,128)(2,1)S(1)} %copy.31) | copy-start | bytes 1572868
  153.8 4.7 %copy-start.5 = (f32[1024,2,512]{2,0,1:T(8,128)S(1)}, f32[1024,2,512]{2,0,1:T(8,128)}, u32[]{:S(2)}) copy-start(f32[1024,2,512]{2,0,1:T(8,128)} %copy-done.4) | copy-start | bytes 12582916
  158.5 2.8 copy-start.11
  160.2 2.3 copy-start.3
  161.0 6.2 %collective-permute-start.7 = (f32[512,128]{1,0:T(8,128)S(1)}, f32[512,128]{1,0:T(8,128)S(1)}, u32[]{:S(2)}, u32[]{:S(2)}) collective-permute-start(f32[512,128]{1,0:T(8,128)S(1)} %constant_dynamic-slice_fusion.1), channel_id=1, source_target_pairs={{0,1},{1,0},{2,3},{3,2},{4,5},{5,4},{6,7},{7,6},{8,9},{9,8},{10,11... | collective-permute-start | bytes 786440 | tf_op jit(solution)/shard_map/ppermute | solution.py:24
  165.6 2.3 collective-permute-start.8
  (1 other events, 1.0 us)
Sparse Core Ops, SparseCore 0:
  9.6 108.6 all-gather.2
  152.9 147.8 reduce-scatter.1
